TPU v7x, 32 devices: a whole 2x2x4 slice. The times are simulated.
32 devices in a mesh: rows: 8 (over z, x), modes: 4 (over y, core).
Axes of the slice: x: 2, y: 2, z: 4, core: 2. Of those that a mesh axis runs over, the one named last changes fastest.
Arguments:
- test_basis: bfloat16 [4096, 5, 256], P('rows'), may hold values from -0.0390625 to 0.0390625
- deim_basis: bfloat16 [4096, 5, 512], P('rows', None, 'modes'), may hold values from -6 to 6
- trial_basis: bfloat16 [4096, 5, 256], P('rows'), may hold values from -6 to 6
- jacobian: float32 [2048, 7, 5], P('rows'), may hold values from -1 to 1
- neighbours: int32 [2048, 7], P('rows'), may hold values from 0 to 4095, as said below
- counts: int32 [8], P('rows'), may hold values from 1 to 256, 512 in all
- sample_inverse: float32 [512, 512], P('modes'), may hold values from -0.01171875 to 0.01171875
Outputs:
- reduced_operator: float32 [256, 256], P('modes', 'rows')
Inputs may be any that keep to these rules, and one draw needn't show every extreme that they name: `neighbours`: the first entry of row g is the sampled cell, which lies among the 512 cells of device g // 256; every other entry lies within 128 cells of it. Device r uses its first counts[r] slots; the counts sum to 512.
All inputs are finite; a program needn't handle non-finite values.
Results may differ from a plain program's by a relative error of at most 0.0003.
Values may be sent and summed in bfloat16 or wider, within the bound.
A program may use at most 64 MiB of HBM per device.

v0:
```python
import jax
import jax.numpy as jnp
from jax import lax
from jax.sharding import PartitionSpec as P

HALO = 128


def entering(part, axis, combine, identity):
    place = lax.axis_index(axis)
    gathered = lax.all_gather(part, axis)
    state = jnp.zeros_like(part) + jnp.asarray(identity, part.dtype)

    def one(turn, state):
        return combine(state, lax.dynamic_index_in_dim(gathered, turn, 0, False))

    return lax.fori_loop(0, place, one, state)


def extended(block, sides, width):
    for axis, dim in sides:
        count = lax.axis_size(axis)
        forward = [(i, i + 1) for i in range(count - 1)]
        backward = [(target, source) for source, target in forward]
        low = lax.ppermute(
            lax.slice_in_dim(block, block.shape[dim] - width, None, axis=dim), axis, forward
        )
        high = lax.ppermute(lax.slice_in_dim(block, 0, width, axis=dim), axis, backward)
        block = jnp.concatenate([low, block, high], axis=dim)
    return block


def add_ints(earlier, later):
    return earlier + later


def shards(test_basis, deim_basis, trial_basis, jacobian, neighbours, counts, sample_inverse):
    cells, comps, width = trial_basis.shape
    slots, coupled = neighbours.shape
    total_modes = sample_inverse.shape[1]
    rank = lax.axis_index("rows")
    groups = lax.axis_size("rows")
    flat_test = test_basis.reshape(cells * comps, width)
    flat_deim = deim_basis.reshape(cells * comps, deim_basis.shape[2])
    partial_g = lax.dot_general(
        flat_test, flat_deim, (((0,), (0,)), ((), ())), preferred_element_type=jnp.float32
    )
    offset = entering(counts, "rows", add_ints, jnp.zeros((1,), jnp.int32))
    slot_ids = jnp.arange(slots, dtype=jnp.int32)
    live = slot_ids < counts[0]
    row_ids = jnp.where(live, offset[0] + slot_ids, -1)
    first_cell = rank * cells
    widened = extended(trial_basis, (("rows", 0),), HALO)
    local = neighbours - (first_cell - HALO)
    picked = widened[local].astype(jnp.float32)
    contrib = jnp.einsum("snj,snjk->sk", jacobian, picked, precision=lax.Precision.HIGHEST)
    mode_ids = jnp.arange(total_modes, dtype=jnp.int32)[None, :]
    total_g = lax.psum(partial_g, "rows")
    folded = jnp.dot(
        total_g, sample_inverse, precision=lax.Precision.HIGHEST, preferred_element_type=jnp.float32
    )
    row_tags = jnp.broadcast_to(row_ids[:, None].astype(jnp.float32), (row_ids.shape[0], groups))
    arrived, arrived_tags = (
        lax.all_to_all(contrib, "rows", split_axis=1, concat_axis=0, tiled=True),
        lax.all_to_all(row_tags, "rows", split_axis=1, concat_axis=0, tiled=True),
    )
    received_ids = arrived_tags[:, 0].astype(jnp.int32)
    selector = (received_ids[:, None] == mode_ids).astype(jnp.float32)
    column_b = lax.dot_general(
        selector,
        arrived,
        (((0,), (0,)), ((), ())),
        precision=lax.Precision.HIGHEST,
        preferred_element_type=jnp.float32,
    )
    column_share = jnp.dot(
        folded, column_b, precision=lax.Precision.HIGHEST, preferred_element_type=jnp.float32
    )
    return lax.psum_scatter(column_share, "modes", scatter_dimension=0, tiled=True)


def solution(mesh):
    in_specs = (
        P("rows", None, None),
        P("rows", None, "modes"),
        P("rows", None, None),
        P("rows", None, None),
        P("rows", None),
        P("rows"),
        P("modes", None),
    )
    out_specs = P("modes", "rows")
    return jax.shard_map(shards, mesh=mesh, in_specs=in_specs, out_specs=out_specs, check_vma=False)
```

profile of v0, /device:TPU:0, one launch (start us, length us, event | category | flops | bytes accessed | tf_op | source)
XLA Modules:
  0.0 193.0 jit_solution(11403932275509942048)
XLA Ops:
  6.5 2.3 %copy.15 = bf16[512,5,256]{2,1,0:T(8,128)(2,1)S(1)} copy(bf16[512,5,256]{2,0,1:T(8,128)(2,1)} %param.11) | data formatting | bytes 2621440 | tf_op args[2]
  8.8 1.1 fusion.3
  9.9 5.7 %collective-permute-start = (bf16[128,5,256]{2,1,0:T(8,128)(2,1)}, bf16[128,5,256]{2,1,0:T(8,128)(2,1)}, u32[]{:S(2)}, u32[]{:S(2)}) collective-permute-start(bf16[128,5,256]{2,1,0:T(8,128)(2,1)} %get-tuple-element.37), channel_id=1, source_target_pairs={{0,4},{4,8},{8,12},{12,16},{16,20},{20,24},{24,28},{1,5},{5,9},{9,... | collective-permute-start | bytes 983048 | tf_op jit(solution)/shard_map/ppermute | solution.py:25
  15.6 1.3 collective-permute-start.1
  17.5 0.6 dynamic-slice
  18.2 0.7 dynamic-update-slice
  18.9 27.9 %all-reduce = s32[8]{0:T(128)S(1)} all-reduce(s32[8]{0:T(128)S(1)} %dynamic-update-slice), channel_id=2, replica_groups=mesh['rows'=8,'modes'=4] {'rows'}, use_global_device_ids=true, to_apply=%add | all-reduce | flops 8 | bytes 64
  46.8 0.6 broadcast_in_dim.16
  47.4 11.0 %all-to-all-start = ((f32[256,8,1]{0,2,1:T(1,128)}), f32[256,8,1]{0,2,1:T(1,128)S(1)}, u32[]{:S(2)}, u32[]{:S(2)}) async-start(f32[256,8,1]{0,2,1:T(1,128)} %broadcast_in_dim.16), calls=%async_computation | async-start | bytes 16384 | tf_op jit(solution)/shard_map/all_to_all | solution.py:65
  58.4 0.1 copy.18
  58.5 0.2 reshape.31
  58.7 1.9 copy.33
  60.7 3.1 %pad_maximum_fusion = bf16[768,5,256]{2,1,0:T(8,128)(2,1)} fusion(bf16[128,5,256]{2,1,0:T(8,128)(2,1)} %collective-permute-done.1, bf16[512,5,256]{2,1,0:T(8,128)(2,1)S(1)} %copy.15, bf16[128,5,256]{2,1,0:T(8,128)(2,1)} %collective-permute-done), kind=kLoop, calls=%fused_computation.5 | loop fusion | flops 1966080 | bytes 3932160 | tf_op jit(solution)/shard_map/concatenate | solution.py:29
  63.8 8.7 %gather_fusion = bf16[1792,5,256]{2,1,0:T(8,128)(2,1)} fusion(bf16[768,5,256]{2,1,0:T(8,128)(2,1)} %pad_maximum_fusion, s32[2048]{0:T(1024)S(1)} %pad_clamp_fusion), kind=kCustom, calls=%fused_computation | custom fusion | bytes 9182208 | tf_op jit(solution)/shard_map/gather | solution.py:55
  72.5 6.0 %multiply_reduce_fusion = f32[256,256]{1,0:T(8,128)S(1)} fusion(f32[256,5,7]{2,0,1:T(8,128)S(1)} %copy-done.1, bf16[256,5,7,256]{3,1,2,0:T(8,128)(2,1)} %bitcast.30), kind=kLoop, calls=%fused_computation.2 | loop fusion | flops 6815744 | bytes 4885504
  78.5 0.8 copy.28
  79.3 6.0 %all-to-all-start.1 = ((f32[256,8,32]{0,2,1:T(8,128)}), f32[256,8,32]{0,2,1:T(8,128)S(1)}, u32[]{:S(2)}, u32[]{:S(2)}) async-start(f32[256,8,32]{0,2,1:T(8,128)} %bitcast.12), calls=%async_computation.1 | async-start | bytes 524288 | tf_op jit(solution)/shard_map/all_to_all | solution.py:64
  85.4 1.2 convolution_bitcast_fusion
  86.7 74.8 %all-reduce.3.cloned.1.call-done = f32[256,128]{1,0:T(8,128)} async-done(((f32[256,128]{1,0:T(8,128)}), f32[256,128]{1,0:T(8,128)}) %all-reduce.3.cloned.1.call-update) | async-done | bytes 131088 | tf_op jit(solution)/shard_map/psum | solution.py:58
  161.5 1.5 fusion.4
  163.0 1.6 fusion
  164.6 1.2 fusion.5
  165.8 18.9 %reduce-scatter.4.cloned.1.call-done = f32[64,32]{1,0:T(8,128)} async-done(((f32[256,32]{1,0:T(8,128)}), f32[64,32]{1,0:T(8,128)}) %reduce-scatter.4.cloned.1.call-update) | async-done | bytes 8208
  184.7 1.4 copy.32
  (27 shorter events, 0.2 us)
Async XLA Ops:
  6.5 78.8 %copy-start = (bf16[512,5,256]{2,0,1:T(8,128)(2,1)S(1)}, bf16[512,5,256]{2,0,1:T(8,128)(2,1)}, u32[]{:S(2)}) copy-start(bf16[512,5,256]{2,0,1:T(8,128)(2,1)} %param.9) | copy-start | bytes 3932164
  6.5 11.0 %copy-start.5 = (u32[32]{0:T(128)S(1)}, u32[32]{0:T(128)}, u32[]{:S(2)}) copy-start(u32[32]{0:T(128)} %constant.31) | copy-start | bytes 388
  6.5 51.8 %copy-start.4 = (s32[256,7]{0,1:T(8,128)S(1)}, s32[256,7]{0,1:T(8,128)}, u32[]{:S(2)}) copy-start(s32[256,7]{0,1:T(8,128)} %param.13) | copy-start | bytes 21508
  9.9 50.7 %collective-permute-start = (bf16[128,5,256]{2,1,0:T(8,128)(2,1)}, bf16[128,5,256]{2,1,0:T(8,128)(2,1)}, u32[]{:S(2)}, u32[]{:S(2)}) collective-permute-start(bf16[128,5,256]{2,1,0:T(8,128)(2,1)} %get-tuple-element.37), channel_id=1, source_target_pairs={{0,4},{4,8},{8,12},{12,16},{16,20},{20,24},{24,28},{1,5},{5,9},{9,... | collective-permute-start | bytes 983048 | tf_op jit(solution)/shard_map/ppermute | solution.py:25
  15.6 45.1 %collective-permute-start.1 = (bf16[128,5,256]{2,1,0:T(8,128)(2,1)}, bf16[128,5,256]{2,1,0:T(8,128)(2,1)}, u32[]{:S(2)}, u32[]{:S(2)}) collective-permute-start(bf16[128,5,256]{2,1,0:T(8,128)(2,1)} %get-tuple-element.38), channel_id=1, source_target_pairs={{4,0},{8,4},{12,8},{16,12},{20,16},{24,20},{28,24},{5,1},{9,5},{13... | collective-permute-start | bytes 983048 | tf_op jit(solution)/shard_map/ppermute | solution.py:28
  47.4 32.0 %all-to-all-start = ((f32[256,8,1]{0,2,1:T(1,128)}), f32[256,8,1]{0,2,1:T(1,128)S(1)}, u32[]{:S(2)}, u32[]{:S(2)}) async-start(f32[256,8,1]{0,2,1:T(1,128)} %broadcast_in_dim.16), calls=%async_computation | async-start | bytes 16384 | tf_op jit(solution)/shard_map/all_to_all | solution.py:65
  63.8 8.7 %copy-start.1 = (f32[256,5,7]{2,0,1:T(8,128)S(1)}, f32[256,5,7]{2,0,1:T(8,128)}, u32[]{:S(2)}) copy-start(f32[256,5,7]{2,0,1:T(8,128)} %copy.33) | copy-start | bytes 107524
  72.5 12.9 %copy-start.2 = (bf16[512,5,128]{2,0,1:T(8,128)(2,1)S(1)}, bf16[512,5,128]{2,0,1:T(8,128)(2,1)}, u32[]{:S(2)}) copy-start(bf16[512,5,128]{2,0,1:T(8,128)(2,1)} %param.10) | copy-start | bytes 1966084
  78.5 83.0 %copy-start.3 = (f32[128,512]{1,0:T(8,128)S(1)}, f32[128,512]{1,0:T(8,128)}, u32[]{:S(2)}) copy-start(f32[128,512]{1,0:T(8,128)} %param.15) | copy-start | bytes 786436
  79.3 83.6 %all-to-all-start.1 = ((f32[256,8,32]{0,2,1:T(8,128)}), f32[256,8,32]{0,2,1:T(8,128)S(1)}, u32[]{:S(2)}, u32[]{:S(2)}) async-start(f32[256,8,32]{0,2,1:T(8,128)} %bitcast.12), calls=%async_computation.1 | async-start | bytes 524288 | tf_op jit(solution)/shard_map/all_to_all | solution.py:64
  85.3 76.1 %all-reduce.3.cloned.1.call-start = ((), (), s32[]{:S(2)}) async-start(), calls=%async_computation.3 | async-start | bytes 262144 | tf_op jit(solution)/shard_map/psum | solution.py:58
  86.6 98.1 %reduce-scatter.4.cloned.1.call-start = ((), (), s32[]{:S(2)}) async-start(), calls=%async_computation.4 | async-start | bytes 163840
Sparse Core Ops, SparseCore 0:
  89.5 71.9 all-reduce.2
  165.9 18.7 reduce-scatter.3
where the time goes:
time: 194 us; the launch traced here: 193 us
  waiting for transfers between devices  93.7 us (48%)
  blocking collectives  27.9 us (14%)
  starting transfers between devices  24 us (12%)
  local copies, waits for them, and re-layouts  18.5 us (10%)
  between operations  14.2 us (7%)
  other arithmetic  9.19 us (5%)
  matrix products  5.49 us (3%)
    psum x1, waiting for transfers between devices, shards(): total_g = lax.psum(partial_g, 'rows')  74.8 us
    unnamed x1, blocking collectives  27.9 us
    unnamed x3, waiting for transfers between devices  18.9 us
    all_to_all x1, starting transfers between devices, shards(): lax.all_to_all(row_tags, 'rows', split_axis=1, concat_axis=0, tiled=True)  11 us
    gather x1, local copies, waits for them, and re-layouts, shards(): picked = widened[local].astype(jnp.float32)  8.66 us
    unnamed x18, local copies, waits for them, and re-layouts  6.97 us
    unnamed x1, other arithmetic  6.03 us
    all_to_all x1, starting transfers between devices, shards(): lax.all_to_all(contrib, 'rows', split_axis=1, concat_axis=0, tiled=True)  5.99 us
  transfers between devices with their start and end apart: 6, of which 2 were waited for; matrix products, arithmetic and copies ran while one was open for 13% of the time, Pallas kernels for 0%

commit v1 on v0

--- a/solution.py
+++ b/solution.py
@@ -1,9 +1,275 @@
+import functools
+
 import jax
 import jax.numpy as jnp
 from jax import lax
+from jax.experimental import pallas as pl
+from jax.experimental.pallas import tpu as pltpu
 from jax.sharding import PartitionSpec as P
 
 HALO = 128
+MESH = pl.DeviceIdType.MESH
+CHUNK = 32
+
+
+def round_up(x, m):
+    return (x + m - 1) // m * m
+
+
+def nt(a, b):
+    return lax.dot_general(
+        a, b, (((1,), (1,)), ((), ())),
+        precision=lax.Precision.HIGHEST, preferred_element_type=jnp.float32,
+    )
+
+
+def tn(a, b):
+    return lax.dot_general(
+        a, b, (((0,), (0,)), ((), ())), preferred_element_type=jnp.float32
+    )
+
+
+def kernel(groups, parts, comps,
+           test_hbm, deim_hbm, trial_hbm, jac_hbm, nbr_hbm, counts_ref, inv_hbm,
+           out_ref,
+           test, deim, trial, inv, jac, nbr, cnt, packed, sparse,
+           g_own, g_in, p_all, s_own, s_in, s_all, o_own, o_in,
+           load_sem, jac_send, jac_recv, nbr_send, nbr_recv, cnt_send, cnt_recv,
+           g_send, g_recv, p_send, p_recv, s_send, s_recv, t_send, t_recv, o_send, o_recv):
+    r = lax.axis_index("rows")
+    m = lax.axis_index("modes")
+    cells = test.shape[0] // comps
+    coupled, slots = nbr.shape[1], nbr.shape[2]
+    modes = deim.shape[1]
+    cols = g_in.shape[1]
+    rows_out = o_own.shape[2]
+    pad = round_up(coupled, 8)
+
+    def peer(t):
+        return lax.rem(r + t, groups)
+
+    def mate(t):
+        return lax.rem(m + t, parts)
+
+    loads = []
+    for j in range(comps):
+        at = pl.ds(j * cells, cells)
+        for i, (src, dst) in enumerate(((test_hbm, test), (deim_hbm, deim), (trial_hbm, trial))):
+            loads.append(pltpu.make_async_copy(src.at[at], dst.at[at], load_sem.at[i, j]))
+    own_jac = pltpu.make_async_copy(jac_hbm, jac.at[1], load_sem.at[3, 0])
+    own_nbr = pltpu.make_async_copy(nbr_hbm, nbr.at[1], load_sem.at[3, 1])
+    own_inv = pltpu.make_async_copy(inv_hbm, inv, load_sem.at[3, 2])
+    own_jac.start()
+    own_nbr.start()
+    for j in range(comps):
+        loads[3 * j].start()
+        loads[3 * j + 1].start()
+    for j in range(comps):
+        loads[3 * j + 2].start()
+    own_inv.start()
+
+    cnt[pl.ds(r, 1)] = jnp.full((1,) + cnt.shape[1:], counts_ref[0], jnp.int32)
+    packed[...] = jnp.zeros_like(packed)
+
+    barrier = pltpu.get_barrier_semaphore()
+    for t in range(1, groups):
+        pl.semaphore_signal(barrier, inc=1, device_id={"rows": peer(t)}, device_id_type=MESH)
+    for t in range(1, parts):
+        pl.semaphore_signal(barrier, inc=1, device_id={"modes": mate(t)}, device_id_type=MESH)
+    pl.semaphore_wait(barrier, groups + parts - 2)
+
+    sent = []
+    small = []
+    for i, t in ((0, 1), (1, groups - 1)):
+        slot = 2 * i
+        for src, dst, ss, rs in ((jac_hbm, jac, jac_send, jac_recv), (nbr_hbm, nbr, nbr_send, nbr_recv)):
+            small.append(pltpu.make_async_remote_copy(
+                src, dst.at[slot], ss.at[i], rs.at[i],
+                device_id={"rows": peer(t)}, device_id_type=MESH))
+    for t in range(1, groups):
+        small.append(pltpu.make_async_remote_copy(
+            cnt.at[r], cnt.at[r], cnt_send.at[t], cnt_recv.at[t],
+            device_id={"rows": peer(t)}, device_id_type=MESH))
+    for c in small:
+        c.start()
+
+    g = jnp.zeros(g_own.shape, jnp.float32)
+    for j in range(comps):
+        loads[3 * j].wait()
+        loads[3 * j + 1].wait()
+        at = pl.ds(j * cells, cells)
+        g += tn(test[at], deim[at])
+    g_own[...] = g
+    g_copies = []
+    for t in range(1, groups):
+        g_copies.append(pltpu.make_async_remote_copy(
+            g_own.at[pl.ds(pl.multiple_of(peer(t) * cols, 8), cols)], g_in.at[r],
+            g_send.at[t], g_recv.at[t],
+            device_id={"rows": peer(t)}, device_id_type=MESH))
+    for c in g_copies:
+        c.start()
+
+    own_jac.wait()
+    own_nbr.wait()
+    for c in small:
+        c.wait()
+    for i in range(3):
+        for j in range(comps):
+            packed[j * pad:j * pad + coupled, i * slots:(i + 1) * slots] = jac[i, j]
+        packed[comps * pad:comps * pad + coupled, i * slots:(i + 1) * slots] = nbr[i].astype(jnp.float32)
+    q_ids = lax.broadcasted_iota(jnp.int32, (slots, modes), 1) + m * modes
+    s_ids = lax.broadcasted_iota(jnp.int32, (slots, modes), 0)
+    picks = []
+    for i in range(3):
+        d = lax.rem(r + i + groups - 1, groups)
+        offset = jnp.zeros((1, modes), jnp.int32)
+        for e in range(groups):
+            offset += jnp.where(e < d, cnt[e, 0:1], 0)
+        held = cnt[d, 0:1]
+        hit = (q_ids - offset == s_ids) & (s_ids < held)
+        picks.append(jnp.where(hit, 1.0, 0.0).astype(jnp.bfloat16))
+    pick = jnp.concatenate(picks, axis=0)
+    x = packed[...]
+    hi = x.astype(jnp.bfloat16)
+    rest = x - hi.astype(jnp.float32)
+    mid = rest.astype(jnp.bfloat16)
+    lo = (rest - mid.astype(jnp.float32)).astype(jnp.bfloat16)
+    split = jnp.concatenate([hi, mid, lo], axis=0)
+    got = lax.dot_general(split, pick, (((1,), (0,)), ((), ())), preferred_element_type=jnp.float32)
+    n = x.shape[0]
+    got = got[:n] + got[n:2 * n] + got[2 * n:]
+
+    near = [got[comps * pad + k:comps * pad + k + 1] - (r * cells).astype(jnp.float32) for k in range(coupled)]
+    entry = [[got[j * pad + k:j * pad + k + 1] for k in range(coupled)] for j in range(comps)]
+    base = lax.broadcasted_iota(jnp.int32, (CHUNK, modes), 0).astype(jnp.float32)
+
+    def build(step, carry):
+        here = base + (step * CHUNK).astype(jnp.float32)
+        acc = [jnp.zeros((CHUNK, modes), jnp.float32) for _ in range(comps)]
+        for k in range(coupled):
+            hit = here == near[k]
+            for j in range(comps):
+                acc[j] += jnp.where(hit, entry[j][k], 0.0)
+        for j in range(comps):
+            hi = acc[j].astype(jnp.bfloat16)
+            lo = (acc[j] - hi.astype(jnp.float32)).astype(jnp.bfloat16)
+            at = pl.ds(pl.multiple_of(j * cells + step * CHUNK, CHUNK), CHUNK)
+            sparse[at, :modes] = hi
+            sparse[at, modes:] = lo
+        return carry
+
+    lax.fori_loop(0, cells // CHUNK, build, 0)
+
+    s = jnp.zeros((trial.shape[1], 2 * modes), jnp.float32)
+    for j in range(comps):
+        loads[3 * j + 2].wait()
+        at = pl.ds(j * cells, cells)
+        s += tn(trial[at], sparse[at])
+    s_own[...] = s[:, :modes] + s[:, modes:]
+    s_copies = []
+    for t in range(1, groups):
+        s_copies.append(pltpu.make_async_remote_copy(
+            s_own.at[pl.ds(pl.multiple_of(peer(t) * cols, 8), cols)], s_in.at[r],
+            s_send.at[t], s_recv.at[t],
+            device_id={"rows": peer(t)}, device_id_type=MESH))
+    for c in s_copies:
+        c.start()
+
+    mine = pl.ds(pl.multiple_of(r * cols, 8), cols)
+    total = g_own[mine]
+    for t in range(1, groups):
+        g_copies[t - 1].wait_recv()
+        total += g_in[lax.rem(r - t + groups, groups)]
+    p_all[mine] = total
+    p_copies = []
+    for t in range(1, groups):
+        p_copies.append(pltpu.make_async_remote_copy(
+            p_all.at[mine], p_all.at[mine], p_send.at[t], p_recv.at[t],
+            device_id={"rows": peer(t)}, device_id_type=MESH))
+    for c in p_copies:
+        c.start()
+
+    total = s_own[mine]
+    for t in range(1, groups):
+        s_copies[t - 1].wait_recv()
+        total += s_in[lax.rem(r - t + groups, groups)]
+    s_all[m] = total
+    t_copies = []
+    for t in range(1, parts):
+        t_copies.append(pltpu.make_async_remote_copy(
+            s_all.at[m], s_all.at[m], t_send.at[t], t_recv.at[t],
+            device_id={"modes": mate(t)}, device_id_type=MESH))
+    for c in t_copies:
+        c.start()
+    own_inv.wait()
+    for c in t_copies:
+        c.wait()
+    folded = jnp.zeros((cols, modes), jnp.float32)
+    for e in range(parts):
+        folded += nt(s_all[e], inv[:, e * modes:(e + 1) * modes])
+    for c in p_copies:
+        c.wait()
+    for e in range(parts):
+        o_own[e] = nt(folded, p_all[e * rows_out:(e + 1) * rows_out])
+    o_copies = []
+    for t in range(1, parts):
+        o_copies.append(pltpu.make_async_remote_copy(
+            o_own.at[mate(t)], o_in.at[m], o_send.at[t], o_recv.at[t],
+            device_id={"modes": mate(t)}, device_id_type=MESH))
+    for c in o_copies:
+        c.start()
+    for c in g_copies + s_copies:
+        c.wait_send()
+    total = o_own[m]
+    for t in range(1, parts):
+        o_copies[t - 1].wait()
+        total += o_in[lax.rem(m - t + parts, parts)]
+    out_ref[...] = total
+
+
+def fused(groups, parts, test_basis, deim_basis, trial_basis, jacobian, neighbours, counts, sample_inverse):
+    cells, comps, width = trial_basis.shape
+    slots, coupled = neighbours.shape
+    modes, total_modes = sample_inverse.shape
+    cols = width // groups
+    rows_out = width // parts
+    flat = lambda b: b.transpose(1, 0, 2).reshape(cells * comps, b.shape[2])
+    f32, bf16, i32 = jnp.float32, jnp.bfloat16, jnp.int32
+    dma = lambda *shape: pltpu.SemaphoreType.DMA(shape)
+    any_spec = pl.BlockSpec(memory_space=pl.ANY)
+    out = pl.pallas_call(
+        functools.partial(kernel, groups, parts, comps),
+        out_shape=jax.ShapeDtypeStruct((cols, rows_out), f32),
+        in_specs=[any_spec] * 5 + [pl.BlockSpec(memory_space=pltpu.SMEM), any_spec],
+        out_specs=pl.BlockSpec(memory_space=pltpu.VMEM),
+        scratch_shapes=[
+            pltpu.VMEM((cells * comps, width), bf16),
+            pltpu.VMEM((cells * comps, modes), bf16),
+            pltpu.VMEM((cells * comps, width), bf16),
+            pltpu.VMEM((modes, total_modes), f32),
+            pltpu.VMEM((3, comps, coupled, slots), f32),
+            pltpu.VMEM((3, coupled, slots), i32),
+            pltpu.VMEM((groups, 8, modes), i32),
+            pltpu.VMEM(((comps + 1) * round_up(coupled, 8), 3 * slots), f32),
+            pltpu.VMEM((cells * comps, 2 * modes), bf16),
+            pltpu.VMEM((width, modes), f32),
+            pltpu.VMEM((groups, cols, modes), f32),
+            pltpu.VMEM((width, modes), f32),
+            pltpu.VMEM((width, modes), f32),
+            pltpu.VMEM((groups, cols, modes), f32),
+            pltpu.VMEM((parts, cols, modes), f32),
+            pltpu.VMEM((parts, cols, rows_out), f32),
+            pltpu.VMEM((parts, cols, rows_out), f32),
+            dma(4, max(comps, 3)), dma(2), dma(2), dma(2), dma(2),
+            dma(groups), dma(groups),
+            dma(groups), dma(groups), dma(groups), dma(groups),
+            dma(groups), dma(groups), dma(parts), dma(parts), dma(parts), dma(parts),
+        ],
+        compiler_params=pltpu.CompilerParams(collective_id=0, has_side_effects=True),
+        name="reduced",
+    )(flat(test_basis), flat(deim_basis), flat(trial_basis), jacobian.transpose(2, 1, 0),
+      neighbours.T, counts, sample_inverse)
+    return out.T
 
 
 def entering(part, axis, combine, identity):
@@ -34,7 +300,7 @@
     return earlier + later
 
 
-def shards(test_basis, deim_basis, trial_basis, jacobian, neighbours, counts, sample_inverse):
+def plain(test_basis, deim_basis, trial_basis, jacobian, neighbours, counts, sample_inverse):
     cells, comps, width = trial_basis.shape
     slots, coupled = neighbours.shape
     total_modes = sample_inverse.shape[1]
@@ -80,6 +346,19 @@
 
 
 def solution(mesh):
+    groups, parts = mesh.shape["rows"], mesh.shape["modes"]
+
+    def shards(*args):
+        cells, comps, width = args[2].shape
+        modes = args[6].shape[0]
+        slots = args[4].shape[0]
+        tiled = (
+            groups >= 3 and parts >= 2 and cells >= HALO
+            and width % (8 * groups) == 0 and width % (8 * parts) == 0
+            and modes % 128 == 0 and slots % 128 == 0 and cells % CHUNK == 0
+        )
+        return fused(groups, parts, *args) if tiled else plain(*args)
+
     in_specs = (
         P("rows", None, None),
         P("rows", None, "modes"),

time: 194 us -> 29 us (0.15)
  waiting for transfers between devices: 93.7 us -> 0 us
  blocking collectives: 27.9 us -> 0 us
  Pallas kernels: 0 us -> 26.7 us
  starting transfers between devices: 24 us -> 0 us
  local copies, waits for them, and re-layouts: 18.5 us -> 1.32 us
  between operations: 14.2 us -> 0.66 us
  other arithmetic: 9.19 us -> 0 us
  matrix products: 5.49 us -> 0 us
    psum x1 -> x0, waiting for transfers between devices: 74.8 us -> none  [shards(): total_g = lax.psum(partial_g, 'rows')]
    unnamed x1 -> x0, blocking collectives: 27.9 us -> none
    pallas_call x0 -> x1, Pallas kernels: none -> 26.7 us  [fused(): pl.pallas_call(functools.partial(kernel, groups, parts, comps), out_shape...]
    unnamed x3 -> x0, waiting for transfers between devices: 18.9 us -> none
    all_to_all x2 -> x0, starting transfers between devices: 17 us -> none  [the longest x1 11 us: shards(): lax.all_to_all(row_tags, 'rows', split_axis=1, concat_axis=0, tiled=True)]
    gather x1 -> x0, local copies, waits for them, and re-layouts: 8.66 us -> none  [shards(): picked = widened[local].astype(jnp.float32)]
    ppermute x2 -> x0, starting transfers between devices: 6.95 us -> none  [the longest x1 5.67 us: extended(): lax.ppermute(lax.slice_in_dim(block, block.shape[dim] - width, None, axis...]
    unnamed x1 -> x0, other arithmetic: 6.03 us -> none
  transfers between devices with their start and end apart: 6 -> 0, of which waited for: 2 -> 0; matrix products, arithmetic and copies ran while one was open for 13% -> 0% of each run, Pallas kernels for 0% -> 0%
where the time goes in v1:
time: 29 us; the launch traced here: 28.7 us
  Pallas kernels  26.7 us (92%)
  local copies, waits for them, and re-layouts  1.32 us (5%)
  between operations  0.66 us (2%)
    pallas_call x1, Pallas kernels, fused(): pl.pallas_call(functools.partial(kernel, groups, parts, comps), out_shape...  26.7 us
    unnamed x1, local copies, waits for them, and re-layouts  1.32 us

profile of v1, /device:TPU:0, one launch (start us, length us, event | category | flops | bytes accessed | tf_op | source)
XLA Modules:
  0.0 28.7 jit_solution(17654364490478008457)
XLA Ops:
  0.7 26.7 %reduced.1 = f32[32,64]{1,0:T(8,128)} custom-call(bf16[2560,256]{1,0:T(8,128)(2,1)} %bitcast.12, bf16[2560,128]{1,0:T(8,128)(2,1)} %bitcast.14, bf16[2560,256]{1,0:T(8,128)(2,1)} %bitcast.13, f32[5,7,256]{2,1,0:T(8,128)} %bitcast.16, s32[7,256]{1,0:T(8,128)} %bitcast.17, s32[1]{0:T(128)S(6)} %copy.9.counts_ref, f32[128,512]{1,0:T(8,128)} %inv_hbm.1), custom_call_target="tpu_custom_call" | custom-call | tf_op jit(solution)/shard_map/reduced/pallas_call | solution.py:240
  27.4 1.3 %copy.10 = f32[64,32]{0,1:T(8,128)} copy(f32[64,32]{0,1:T(8,128)} %bitcast.15) | data formatting | bytes 16384

commit v2 on v1

--- a/solution.py
+++ b/solution.py
@@ -16,11 +16,17 @@
     return (x + m - 1) // m * m
 
 
-def nt(a, b):
-    return lax.dot_general(
-        a, b, (((1,), (1,)), ((), ())),
-        precision=lax.Precision.HIGHEST, preferred_element_type=jnp.float32,
-    )
+def pieces(x):
+    hi = x.astype(jnp.bfloat16)
+    return hi, (x - hi.astype(jnp.float32)).astype(jnp.bfloat16)
+
+
+def nt_split(a, b):
+    rows = a[0].shape[0]
+    contract = (((1,), (1,)), ((), ()))
+    main = lax.dot_general(jnp.concatenate(a, axis=0), b[0], contract, preferred_element_type=jnp.float32)
+    rest = lax.dot_general(a[0], b[1], contract, preferred_element_type=jnp.float32)
+    return main[:rows] + (main[rows:] + rest)
 
 
 def tn(a, b):
@@ -29,35 +35,55 @@
     )
 
 
-def kernel(groups, parts, comps,
+def kernel(groups, parts, comps, coupled,
            test_hbm, deim_hbm, trial_hbm, jac_hbm, nbr_hbm, counts_ref, inv_hbm,
            out_ref,
-           test, deim, trial, inv, jac, nbr, cnt, packed, sparse,
-           g_own, g_in, p_all, s_own, s_in, s_all, o_own, o_in,
-           load_sem, jac_send, jac_recv, nbr_send, nbr_recv, cnt_send, cnt_recv,
+           test, deim, trial, inv, jac, nbr, cnt, slot_data, turned, sparse,
+           g_own, g_in, p_all, p_hi, p_lo, s_own, s_in, s_all, inv_hi, inv_lo, o_own, o_in,
+           load_sem, slot_send, slot_recv, cnt_send, cnt_recv,
            g_send, g_recv, p_send, p_recv, s_send, s_recv, t_send, t_recv, o_send, o_recv):
     r = lax.axis_index("rows")
     m = lax.axis_index("modes")
     cells = test.shape[0] // comps
-    coupled, slots = nbr.shape[1], nbr.shape[2]
+    slots = nbr.shape[1]
     modes = deim.shape[1]
     cols = g_in.shape[1]
     rows_out = o_own.shape[2]
     pad = round_up(coupled, 8)
+    far_first = sorted(range(1, groups), key=lambda t: -min(t, groups - t))
 
     def peer(t):
         return lax.rem(r + t, groups)
 
     def mate(t):
         return lax.rem(m + t, parts)
+
+    def to_peer(src, dst, send, recv, t):
+        return pltpu.make_async_remote_copy(
+            src, dst, send.at[t], recv.at[t], device_id={"rows": peer(t)}, device_id_type=MESH)
+
+    def to_mate(src, dst, send, recv, t):
+        return pltpu.make_async_remote_copy(
+            src, dst, send.at[t], recv.at[t], device_id={"modes": mate(t)}, device_id_type=MESH)
+
+    def block(t):
+        return pl.ds(pl.multiple_of(peer(t) * cols, 8), cols)
+
+    mine = pl.ds(pl.multiple_of(r * cols, 8), cols)
+
+    barrier = pltpu.get_barrier_semaphore()
+    for t in far_first:
+        pl.semaphore_signal(barrier, inc=1, device_id={"rows": peer(t)}, device_id_type=MESH)
+    for t in range(1, parts):
+        pl.semaphore_signal(barrier, inc=1, device_id={"modes": mate(t)}, device_id_type=MESH)
 
     loads = []
     for j in range(comps):
         at = pl.ds(j * cells, cells)
         for i, (src, dst) in enumerate(((test_hbm, test), (deim_hbm, deim), (trial_hbm, trial))):
             loads.append(pltpu.make_async_copy(src.at[at], dst.at[at], load_sem.at[i, j]))
-    own_jac = pltpu.make_async_copy(jac_hbm, jac.at[1], load_sem.at[3, 0])
-    own_nbr = pltpu.make_async_copy(nbr_hbm, nbr.at[1], load_sem.at[3, 1])
+    own_jac = pltpu.make_async_copy(jac_hbm, jac, load_sem.at[3, 0])
+    own_nbr = pltpu.make_async_copy(nbr_hbm, nbr, load_sem.at[3, 1])
     own_inv = pltpu.make_async_copy(inv_hbm, inv, load_sem.at[3, 2])
     own_jac.start()
     own_nbr.start()
@@ -69,30 +95,12 @@
     own_inv.start()
 
     cnt[pl.ds(r, 1)] = jnp.full((1,) + cnt.shape[1:], counts_ref[0], jnp.int32)
-    packed[...] = jnp.zeros_like(packed)
-
-    barrier = pltpu.get_barrier_semaphore()
-    for t in range(1, groups):
-        pl.semaphore_signal(barrier, inc=1, device_id={"rows": peer(t)}, device_id_type=MESH)
-    for t in range(1, parts):
-        pl.semaphore_signal(barrier, inc=1, device_id={"modes": mate(t)}, device_id_type=MESH)
-    pl.semaphore_wait(barrier, groups + parts - 2)
-
-    sent = []
-    small = []
-    for i, t in ((0, 1), (1, groups - 1)):
-        slot = 2 * i
-        for src, dst, ss, rs in ((jac_hbm, jac, jac_send, jac_recv), (nbr_hbm, nbr, nbr_send, nbr_recv)):
-            small.append(pltpu.make_async_remote_copy(
-                src, dst.at[slot], ss.at[i], rs.at[i],
-                device_id={"rows": peer(t)}, device_id_type=MESH))
-    for t in range(1, groups):
-        small.append(pltpu.make_async_remote_copy(
-            cnt.at[r], cnt.at[r], cnt_send.at[t], cnt_recv.at[t],
-            device_id={"rows": peer(t)}, device_id_type=MESH))
-    for c in small:
-        c.start()
-
+    own_jac.wait()
+    own_nbr.wait()
+    slot_data[1] = jnp.zeros(slot_data.shape[1:], jnp.float32)
+    for j in range(comps):
+        slot_data[1, j * pad:j * pad + coupled] = jac[j]
+    slot_data[1, comps * pad:comps * pad + coupled] = nbr[...].astype(jnp.float32)
     g = jnp.zeros(g_own.shape, jnp.float32)
     for j in range(comps):
         loads[3 * j].wait()
@@ -100,43 +108,50 @@
         at = pl.ds(j * cells, cells)
         g += tn(test[at], deim[at])
     g_own[...] = g
-    g_copies = []
-    for t in range(1, groups):
-        g_copies.append(pltpu.make_async_remote_copy(
-            g_own.at[pl.ds(pl.multiple_of(peer(t) * cols, 8), cols)], g_in.at[r],
-            g_send.at[t], g_recv.at[t],
+
+    pl.semaphore_wait(barrier, groups + parts - 2)
+
+    small = []
+    for i, t in ((0, 1), (1, groups - 1)):
+        small.append(pltpu.make_async_remote_copy(
+            slot_data.at[1], slot_data.at[2 * i],
+            slot_send.at[i], slot_recv.at[i],
             device_id={"rows": peer(t)}, device_id_type=MESH))
+    small += [to_peer(cnt.at[r], cnt.at[r], cnt_send, cnt_recv, t) for t in far_first]
+    for c in small:
+        c.start()
+    g_copies = [to_peer(g_own.at[block(t)], g_in.at[r], g_send, g_recv, t) for t in far_first]
     for c in g_copies:
         c.start()
 
-    own_jac.wait()
-    own_nbr.wait()
+    for j in range(comps):
+        loads[3 * j + 2].wait()
+        at = pl.ds(j * cells, cells)
+        turned[:, at] = trial[at].T
+    own_inv.wait()
+    for e in range(parts):
+        inv_hi[e], inv_lo[e] = pieces(inv[:, e * modes:(e + 1) * modes])
+
     for c in small:
         c.wait()
-    for i in range(3):
-        for j in range(comps):
-            packed[j * pad:j * pad + coupled, i * slots:(i + 1) * slots] = jac[i, j]
-        packed[comps * pad:comps * pad + coupled, i * slots:(i + 1) * slots] = nbr[i].astype(jnp.float32)
     q_ids = lax.broadcasted_iota(jnp.int32, (slots, modes), 1) + m * modes
     s_ids = lax.broadcasted_iota(jnp.int32, (slots, modes), 0)
-    picks = []
+    n = slot_data.shape[1]
+    got = jnp.zeros((3 * n, modes), jnp.float32)
     for i in range(3):
         d = lax.rem(r + i + groups - 1, groups)
         offset = jnp.zeros((1, modes), jnp.int32)
         for e in range(groups):
             offset += jnp.where(e < d, cnt[e, 0:1], 0)
-        held = cnt[d, 0:1]
-        hit = (q_ids - offset == s_ids) & (s_ids < held)
-        picks.append(jnp.where(hit, 1.0, 0.0).astype(jnp.bfloat16))
-    pick = jnp.concatenate(picks, axis=0)
-    x = packed[...]
-    hi = x.astype(jnp.bfloat16)
-    rest = x - hi.astype(jnp.float32)
-    mid = rest.astype(jnp.bfloat16)
-    lo = (rest - mid.astype(jnp.float32)).astype(jnp.bfloat16)
-    split = jnp.concatenate([hi, mid, lo], axis=0)
-    got = lax.dot_general(split, pick, (((1,), (0,)), ((), ())), preferred_element_type=jnp.float32)
-    n = x.shape[0]
+        hit = (q_ids - offset == s_ids) & (s_ids < cnt[d, 0:1])
+        pick = jnp.where(hit, 1.0, 0.0).astype(jnp.bfloat16)
+        x = slot_data[i]
+        hi = x.astype(jnp.bfloat16)
+        rest = x - hi.astype(jnp.float32)
+        mid = rest.astype(jnp.bfloat16)
+        lo = (rest - mid.astype(jnp.float32)).astype(jnp.bfloat16)
+        split = jnp.concatenate([hi, mid, lo], axis=0)
+        got += lax.dot_general(split, pick, (((1,), (0,)), ((), ())), preferred_element_type=jnp.float32)
     got = got[:n] + got[n:2 * n] + got[2 * n:]
 
     near = [got[comps * pad + k:comps * pad + k + 1] - (r * cells).astype(jnp.float32) for k in range(coupled)]
@@ -160,62 +175,43 @@
 
     lax.fori_loop(0, cells // CHUNK, build, 0)
 
-    s = jnp.zeros((trial.shape[1], 2 * modes), jnp.float32)
-    for j in range(comps):
-        loads[3 * j + 2].wait()
-        at = pl.ds(j * cells, cells)
-        s += tn(trial[at], sparse[at])
+    s = lax.dot_general(
+        turned[...], sparse[...], (((1,), (0,)), ((), ())), preferred_element_type=jnp.float32)
     s_own[...] = s[:, :modes] + s[:, modes:]
-    s_copies = []
-    for t in range(1, groups):
-        s_copies.append(pltpu.make_async_remote_copy(
-            s_own.at[pl.ds(pl.multiple_of(peer(t) * cols, 8), cols)], s_in.at[r],
-            s_send.at[t], s_recv.at[t],
-            device_id={"rows": peer(t)}, device_id_type=MESH))
+    s_copies = [to_peer(s_own.at[block(t)], s_in.at[r], s_send, s_recv, t) for t in far_first]
     for c in s_copies:
         c.start()
 
-    mine = pl.ds(pl.multiple_of(r * cols, 8), cols)
     total = g_own[mine]
-    for t in range(1, groups):
-        g_copies[t - 1].wait_recv()
+    for t, c in zip(far_first, g_copies):
+        c.wait_recv()
         total += g_in[lax.rem(r - t + groups, groups)]
     p_all[mine] = total
-    p_copies = []
-    for t in range(1, groups):
-        p_copies.append(pltpu.make_async_remote_copy(
-            p_all.at[mine], p_all.at[mine], p_send.at[t], p_recv.at[t],
-            device_id={"rows": peer(t)}, device_id_type=MESH))
+    p_copies = [to_peer(p_all.at[mine], p_all.at[mine], p_send, p_recv, t) for t in far_first]
     for c in p_copies:
         c.start()
 
     total = s_own[mine]
-    for t in range(1, groups):
-        s_copies[t - 1].wait_recv()
+    for t, c in zip(far_first, s_copies):
+        c.wait_recv()
         total += s_in[lax.rem(r - t + groups, groups)]
     s_all[m] = total
-    t_copies = []
-    for t in range(1, parts):
-        t_copies.append(pltpu.make_async_remote_copy(
-            s_all.at[m], s_all.at[m], t_send.at[t], t_recv.at[t],
-            device_id={"modes": mate(t)}, device_id_type=MESH))
+    t_copies = [to_mate(s_all.at[m], s_all.at[m], t_send, t_recv, t) for t in range(1, parts)]
     for c in t_copies:
         c.start()
-    own_inv.wait()
-    for c in t_copies:
-        c.wait()
-    folded = jnp.zeros((cols, modes), jnp.float32)
-    for e in range(parts):
-        folded += nt(s_all[e], inv[:, e * modes:(e + 1) * modes])
+    folded = nt_split(pieces(total), (inv_hi[m], inv_lo[m]))
     for c in p_copies:
         c.wait()
     for e in range(parts):
-        o_own[e] = nt(folded, p_all[e * rows_out:(e + 1) * rows_out])
-    o_copies = []
-    for t in range(1, parts):
-        o_copies.append(pltpu.make_async_remote_copy(
-            o_own.at[mate(t)], o_in.at[m], o_send.at[t], o_recv.at[t],
-            device_id={"modes": mate(t)}, device_id_type=MESH))
+        p_hi[e], p_lo[e] = pieces(p_all[e * rows_out:(e + 1) * rows_out])
+    for t, c in zip(range(1, parts), t_copies):
+        c.wait()
+        e = lax.rem(m - t + parts, parts)
+        folded += nt_split(pieces(s_all[e]), (inv_hi[e], inv_lo[e]))
+    folded = pieces(folded)
+    for e in range(parts):
+        o_own[e] = nt_split(folded, (p_hi[e], p_lo[e]))
+    o_copies = [to_mate(o_own.at[mate(t)], o_in.at[m], o_send, o_recv, t) for t in range(1, parts)]
     for c in o_copies:
         c.start()
     for c in g_copies + s_copies:
@@ -238,7 +234,7 @@
     dma = lambda *shape: pltpu.SemaphoreType.DMA(shape)
     any_spec = pl.BlockSpec(memory_space=pl.ANY)
     out = pl.pallas_call(
-        functools.partial(kernel, groups, parts, comps),
+        functools.partial(kernel, groups, parts, comps, coupled),
         out_shape=jax.ShapeDtypeStruct((cols, rows_out), f32),
         in_specs=[any_spec] * 5 + [pl.BlockSpec(memory_space=pltpu.SMEM), any_spec],
         out_specs=pl.BlockSpec(memory_space=pltpu.VMEM),
@@ -247,21 +243,25 @@
             pltpu.VMEM((cells * comps, modes), bf16),
             pltpu.VMEM((cells * comps, width), bf16),
             pltpu.VMEM((modes, total_modes), f32),
-            pltpu.VMEM((3, comps, coupled, slots), f32),
-            pltpu.VMEM((3, coupled, slots), i32),
+            pltpu.VMEM((comps, coupled, slots), f32),
+            pltpu.VMEM((coupled, slots), i32),
             pltpu.VMEM((groups, 8, modes), i32),
-            pltpu.VMEM(((comps + 1) * round_up(coupled, 8), 3 * slots), f32),
+            pltpu.VMEM((3, (comps + 1) * round_up(coupled, 8), slots), f32),
+            pltpu.VMEM((width, cells * comps), bf16),
             pltpu.VMEM((cells * comps, 2 * modes), bf16),
             pltpu.VMEM((width, modes), f32),
             pltpu.VMEM((groups, cols, modes), f32),
             pltpu.VMEM((width, modes), f32),
+            pltpu.VMEM((parts, rows_out, modes), bf16),
+            pltpu.VMEM((parts, rows_out, modes), bf16),
             pltpu.VMEM((width, modes), f32),
             pltpu.VMEM((groups, cols, modes), f32),
             pltpu.VMEM((parts, cols, modes), f32),
+            pltpu.VMEM((parts, modes, modes), bf16),
+            pltpu.VMEM((parts, modes, modes), bf16),
             pltpu.VMEM((parts, cols, rows_out), f32),
             pltpu.VMEM((parts, cols, rows_out), f32),
-            dma(4, max(comps, 3)), dma(2), dma(2), dma(2), dma(2),
-            dma(groups), dma(groups),
+            dma(4, max(comps, 3)), dma(2), dma(2), dma(groups), dma(groups),
             dma(groups), dma(groups), dma(groups), dma(groups),
             dma(groups), dma(groups), dma(parts), dma(parts), dma(parts), dma(parts),
         ],
@@ -354,7 +354,7 @@
         slots = args[4].shape[0]
         tiled = (
             groups >= 3 and parts >= 2 and cells >= HALO
-            and width % (8 * groups) == 0 and width % (8 * parts) == 0
+            and width % (8 * groups) == 0 and width % 128 == 0 and width % (16 * parts) == 0
             and modes % 128 == 0 and slots % 128 == 0 and cells % CHUNK == 0
         )
         return fused(groups, parts, *args) if tiled else plain(*args)

time: 29 us -> 28.2 us (0.972)
  Pallas kernels: 26.7 us -> 26 us
    pallas_call x1, Pallas kernels: 26.7 us -> 26 us  [fused(): pl.pallas_call(functools.partial(kernel, groups, parts, comps, coupled),...]
where the time goes in v2:
time: 28.2 us; the launch traced here: 28 us
  Pallas kernels  26 us (92%)
  local copies, waits for them, and re-layouts  1.32 us (5%)
  between operations  0.66 us (2%)
    pallas_call x1, Pallas kernels, fused(): pl.pallas_call(functools.partial(kernel, groups, parts, comps, coupled),...  26 us
    unnamed x1, local copies, waits for them, and re-layouts  1.32 us

profile of v2, /device:TPU:0, one launch (start us, length us, event | category | flops | bytes accessed | tf_op | source)
XLA Modules:
  0.0 28.0 jit_solution(13674811576818180823)
XLA Ops:
  0.7 26.0 %reduced.1 = f32[32,64]{1,0:T(8,128)} custom-call(bf16[2560,256]{1,0:T(8,128)(2,1)} %bitcast.12, bf16[2560,128]{1,0:T(8,128)(2,1)} %bitcast.14, bf16[2560,256]{1,0:T(8,128)(2,1)} %bitcast.13, f32[5,7,256]{2,1,0:T(8,128)} %bitcast.16, s32[7,256]{1,0:T(8,128)} %bitcast.17, s32[1]{0:T(128)S(6)} %copy.9.counts_ref, f32[128,512]{1,0:T(8,128)} %inv_hbm.1), custom_call_target="tpu_custom_call" | custom-call | tf_op jit(solution)/shard_map/reduced/pallas_call | solution.py:236
  26.7 1.3 %copy.10 = f32[64,32]{0,1:T(8,128)} copy(f32[64,32]{0,1:T(8,128)} %bitcast.15) | data formatting | bytes 16384
